TPU v7x, 32 devices: a whole 2x2x4 slice. The times are simulated.
32 devices in a mesh: dp: 8 (over z, y), tensor: 4 (over x, core).
Axes of the slice: x: 2, y: 2, z: 4, core: 2. Of those that a mesh axis runs over, the one named last changes fastest.
Arguments:
- tokens: bfloat16 [24, 736, 768], P('dp', None, 'tensor'), may hold values from -6 to 6
- horizon: int32 [24], P('dp'), may hold values from 4 to 30, as said below
- attn_gain: float32 [768], replicated, may hold values from 0.5 to 1.5
- attn_shift: float32 [768], replicated, may hold values from -1.5 to 1.5
- query_weight: bfloat16 [768, 768], P(None, 'tensor'), may hold values from -0.21875 to 0.21875
- key_weight: bfloat16 [768, 768], P(None, 'tensor'), may hold values from -0.21875 to 0.21875
- value_weight: bfloat16 [768, 768], P(None, 'tensor'), may hold values from -0.21875 to 0.21875
- query_bias: float32 [768], P('tensor'), may hold values from -2.5 to 2.5
- value_bias: float32 [768], P('tensor'), may hold values from -2.5 to 2.5
- output_weight: bfloat16 [768, 768], P('tensor'), may hold values from -0.625 to 0.625
- output_bias: float32 [768], P('tensor'), may hold values from -1.5 to 1.5
- mlp_gain: float32 [768], replicated, may hold values from 0.5 to 1.5
- mlp_shift: float32 [768], replicated, may hold values from -1.5 to 1.5
- up_weight: bfloat16 [768, 3072], P(None, 'tensor'), may hold values from -0.21875 to 0.21875
- up_bias: float32 [3072], P('tensor'), may hold values from -2.5 to 2.5
- down_weight: bfloat16 [3072, 768], P('tensor'), may hold values from -0.15625 to 0.15625
- down_bias: float32 [768], P('tensor'), may hold values from -1.5 to 1.5
- cotangent: bfloat16 [24, 736, 768], P('dp', None, 'tensor'), may hold values from -6 to 6
Outputs:
- result: bfloat16 [24, 736, 768], P('dp', None, 'tensor')
- grad_tokens: bfloat16 [24, 736, 768], P('dp', None, 'tensor')
- grad_attn_gain: float32 [768], P('tensor')
- grad_attn_shift: float32 [768], P('tensor')
- grad_query_weight: float32 [768, 768], P(None, 'tensor')
- grad_key_weight: float32 [768, 768], P(None, 'tensor')
- grad_value_weight: float32 [768, 768], P(None, 'tensor')
- grad_query_bias: float32 [768], P('tensor')
- grad_value_bias: float32 [768], P('tensor')
- grad_output_weight: float32 [768, 768], P('tensor')
- grad_output_bias: float32 [768], P('tensor')
- grad_mlp_gain: float32 [768], P('tensor')
- grad_mlp_shift: float32 [768], P('tensor')
- grad_up_weight: float32 [768, 3072], P(None, 'tensor')
- grad_up_bias: float32 [3072], P('tensor')
- grad_down_weight: float32 [3072, 768], P('tensor')
- grad_down_bias: float32 [768], P('tensor')
Inputs may be any that keep to these rules, and one draw needn't show every extreme that they name: horizon[c] is the number of future frames of clip c; the clip's first 256 + 16 * horizon[c] rows are real, the rest of its 736 rows are padding.
All inputs are finite; a program needn't handle non-finite values.
Results may differ from a plain program's by a relative error of at most 0.012.
Values may be sent and summed in bfloat16 or wider, within the bound.
No kernel may reach another device: no remote copies, remote signals or barrier semaphores. Data moves between devices by JAX's collectives and lax.ppermute only.
A program may use at most 192 MiB of HBM per device.

v0:
```python
from functools import partial
import jax
import jax.numpy as jnp
from jax import lax
from jax.sharding import PartitionSpec as P

HDIM = 64
CONTEXT = 256
FRAME = 16
EPS = 1e-05
NEGATIVE = -1e30


def matmul(left, right):
    return jnp.dot(left, right, preferred_element_type=jnp.float32)


def inner_rows(left, right):
    return lax.dot_general(
        left, right, (((0,), (0,)), ((), ())), preferred_element_type=jnp.float32
    )


def times_transposed(left, right):
    return lax.dot_general(
        left, right, (((1,), (1,)), ((), ())), preferred_element_type=jnp.float32
    )


def normalize(rows):
    row_mean = jnp.mean(rows, axis=1, keepdims=True)
    centered = rows - row_mean
    row_var = jnp.mean(centered * centered, axis=1, keepdims=True)
    inv_std = lax.rsqrt(row_var + EPS)
    return (centered * inv_std, inv_std)


def clip_mask(clip_rows, length):
    position = jnp.arange(clip_rows, dtype=jnp.int32)
    return (position[None, :] <= position[:, None]) & (position[None, :] < length)


def clip_scores(query_clip, key_clip, length):
    factor = query_clip.shape[-1] ** (-0.5)
    scores = (
        jnp.einsum("qhd,khd->hqk", query_clip, key_clip, preferred_element_type=jnp.float32)
        * factor
    )
    allowed = clip_mask(query_clip.shape[0], length)
    return (jnp.where(allowed[None], scores, NEGATIVE), allowed, factor)


def attend_forward(pieces):
    query_clip, key_clip, value_clip, length = pieces
    scores, allowed, factor = clip_scores(query_clip, key_clip, length)
    row_max = jnp.max(scores, axis=2, keepdims=True)
    exp_terms = jnp.exp(scores - row_max)
    row_total = jnp.sum(exp_terms, axis=2, keepdims=True)
    attn_prob = (exp_terms / row_total).astype(jnp.bfloat16)
    mixed = jnp.einsum("hqk,khd->qhd", attn_prob, value_clip, preferred_element_type=jnp.float32)
    return (mixed.astype(jnp.bfloat16), (row_max + jnp.log(row_total))[:, :, 0])


def attend_backward(pieces):
    query_clip, key_clip, value_clip, grad_mixed, log_total, length = pieces
    scores, allowed, factor = clip_scores(query_clip, key_clip, length)
    attn_prob = jnp.where(allowed[None], jnp.exp(scores - log_total[:, :, None]), 0.0)
    grad_value = jnp.einsum(
        "hqk,qhd->khd",
        attn_prob.astype(jnp.bfloat16),
        grad_mixed,
        preferred_element_type=jnp.float32,
    ).astype(jnp.bfloat16)
    grad_prob = jnp.einsum(
        "qhd,khd->hqk", grad_mixed, value_clip, preferred_element_type=jnp.float32
    )
    row_delta = jnp.sum(attn_prob * grad_prob, axis=2, keepdims=True)
    grad_score = (attn_prob * (grad_prob - row_delta)).astype(jnp.bfloat16)
    grad_query = (
        jnp.einsum("hqk,khd->qhd", grad_score, key_clip, preferred_element_type=jnp.float32)
        * factor
    ).astype(jnp.bfloat16)
    grad_key = (
        jnp.einsum("hqk,qhd->khd", grad_score, query_clip, preferred_element_type=jnp.float32)
        * factor
    ).astype(jnp.bfloat16)
    return (grad_query, grad_key, grad_value)


def norm_back(grad_part, normed, inv_std, gain, own_start, own_width):
    grad_norm = lax.psum(grad_part, "tensor")
    scaled = grad_norm * gain
    first_mean = jnp.mean(scaled, axis=1, keepdims=True)
    second_mean = jnp.mean(scaled * normed, axis=1, keepdims=True)
    grad_full = inv_std * (scaled - first_mean - normed * second_mean)
    grad_in = lax.dynamic_slice_in_dim(grad_full, own_start, own_width, 1)
    grad_own = lax.dynamic_slice_in_dim(grad_norm, own_start, own_width, 1)
    normed_own = lax.dynamic_slice_in_dim(normed, own_start, own_width, 1)
    grad_gain = jnp.sum(grad_own * normed_own, axis=0)
    grad_shift = jnp.sum(grad_own, axis=0)
    return (grad_in, grad_gain, grad_shift)


def local(
    tokens,
    horizon,
    attn_gain,
    attn_shift,
    query_weight,
    key_weight,
    value_weight,
    query_bias,
    value_bias,
    output_weight,
    output_bias,
    mlp_gain,
    mlp_shift,
    up_weight,
    up_bias,
    down_weight,
    down_bias,
    cotangent,
):
    clip_count, clip_rows, own_width = tokens.shape
    row_count = clip_count * clip_rows
    own_start = lax.axis_index("tensor") * own_width
    lengths = CONTEXT + FRAME * horizon
    gathered = (
        lax.all_gather(tokens, "tensor", axis=2, tiled=True)
        .reshape(row_count, -1)
        .astype(jnp.float32)
    )
    normed_one, inv_one = normalize(gathered)
    acts_one = (normed_one * attn_gain + attn_shift).astype(jnp.bfloat16)
    queries = (matmul(acts_one, query_weight) + query_bias).astype(jnp.bfloat16)
    keys_all = matmul(acts_one, key_weight).astype(jnp.bfloat16)
    values = (matmul(acts_one, value_weight) + value_bias).astype(jnp.bfloat16)
    head_count = queries.shape[1] // HDIM
    shaped = (clip_count, clip_rows, head_count, HDIM)
    query_four = queries.reshape(shaped)
    key_four = keys_all.reshape(shaped)
    value_four = values.reshape(shaped)
    mixed, log_total = lax.map(attend_forward, (query_four, key_four, value_four, lengths))
    mixed = mixed.reshape(row_count, -1)
    attn_own = lax.psum_scatter(
        matmul(mixed, output_weight), "tensor", scatter_dimension=1, tiled=True
    )
    middle = tokens.reshape(row_count, own_width).astype(jnp.float32) + attn_own + output_bias
    middle_all = lax.all_gather(middle.astype(jnp.bfloat16), "tensor", axis=1, tiled=True).astype(
        jnp.float32
    )
    normed_two, inv_two = normalize(middle_all)
    acts_two = (normed_two * mlp_gain + mlp_shift).astype(jnp.bfloat16)
    hidden_pre = matmul(acts_two, up_weight) + up_bias
    hidden_full, gelu_back = jax.vjp(partial(jax.nn.gelu, approximate=True), hidden_pre)
    hidden = hidden_full.astype(jnp.bfloat16)
    mlp_own = lax.psum_scatter(
        matmul(hidden, down_weight).astype(jnp.bfloat16), "tensor", scatter_dimension=1, tiled=True
    ).astype(jnp.float32)
    result = (
        (middle + mlp_own + down_bias)
        .astype(jnp.bfloat16)
        .reshape(clip_count, clip_rows, own_width)
    )
    valid = (jnp.arange(clip_rows, dtype=jnp.int32)[None, :] < lengths[:, None]).astype(jnp.float32)
    grad_out = (cotangent.astype(jnp.float32) * valid[:, :, None]).reshape(row_count, own_width)
    grad_all = lax.all_gather(grad_out.astype(jnp.bfloat16), "tensor", axis=1, tiled=True)
    grad_down_bias = jnp.sum(grad_out, axis=0)
    grad_down_weight = inner_rows(hidden, grad_all)
    grad_hidden = times_transposed(grad_all, down_weight)
    grad_pre = gelu_back(grad_hidden)[0].astype(jnp.bfloat16)
    grad_up_bias = jnp.sum(grad_pre.astype(jnp.float32), axis=0)
    grad_up_weight = inner_rows(acts_two, grad_pre)
    back_two, grad_mlp_gain, grad_mlp_shift = norm_back(
        times_transposed(grad_pre, up_weight), normed_two, inv_two, mlp_gain, own_start, own_width
    )
    grad_middle = grad_out + back_two
    grad_mid_all = lax.all_gather(grad_middle.astype(jnp.bfloat16), "tensor", axis=1, tiled=True)
    grad_output_bias = jnp.sum(grad_middle, axis=0)
    grad_output_weight = inner_rows(mixed, grad_mid_all)
    grad_mixed = times_transposed(grad_mid_all, output_weight).astype(jnp.bfloat16)
    grad_query, grad_key, grad_value = lax.map(
        attend_backward,
        (query_four, key_four, value_four, grad_mixed.reshape(shaped), log_total, lengths),
    )
    grad_query = grad_query.reshape(row_count, -1)
    grad_key = grad_key.reshape(row_count, -1)
    grad_value = grad_value.reshape(row_count, -1)
    grad_query_bias = jnp.sum(grad_query.astype(jnp.float32), axis=0)
    grad_value_bias = jnp.sum(grad_value.astype(jnp.float32), axis=0)
    grad_query_weight = inner_rows(acts_one, grad_query)
    grad_key_weight = inner_rows(acts_one, grad_key)
    grad_value_weight = inner_rows(acts_one, grad_value)
    back_in = (
        times_transposed(grad_query, query_weight)
        + times_transposed(grad_key, key_weight)
        + times_transposed(grad_value, value_weight)
    )
    back_one, grad_attn_gain, grad_attn_shift = norm_back(
        back_in, normed_one, inv_one, attn_gain, own_start, own_width
    )
    grad_rows = (
        (grad_middle + back_one).astype(jnp.bfloat16).reshape(clip_count, clip_rows, own_width)
    )
    summed = lax.psum(
        (
            grad_attn_gain,
            grad_attn_shift,
            grad_query_weight,
            grad_key_weight,
            grad_value_weight,
            grad_query_bias,
            grad_value_bias,
            grad_output_weight,
            grad_output_bias,
            grad_mlp_gain,
            grad_mlp_shift,
            grad_up_weight,
            grad_up_bias,
            grad_down_weight,
            grad_down_bias,
        ),
        "dp",
    )
    return (result, grad_rows) + tuple(summed)


def solution(mesh):
    placed = (
        P("dp", None, "tensor"),
        P("dp"),
        P(),
        P(),
        P(None, "tensor"),
        P(None, "tensor"),
        P(None, "tensor"),
        P("tensor"),
        P("tensor"),
        P("tensor", None),
        P("tensor"),
        P(),
        P(),
        P(None, "tensor"),
        P("tensor"),
        P("tensor", None),
        P("tensor"),
        P("dp", None, "tensor"),
    )
    return jax.shard_map(
        local,
        mesh=mesh,
        in_specs=placed,
        out_specs=(
            P("dp", None, "tensor"),
            P("dp", None, "tensor"),
            P("tensor"),
            P("tensor"),
            P(None, "tensor"),
            P(None, "tensor"),
            P(None, "tensor"),
            P("tensor"),
            P("tensor"),
            P("tensor", None),
            P("tensor"),
            P("tensor"),
            P("tensor"),
            P(None, "tensor"),
            P("tensor"),
            P("tensor", None),
            P("tensor"),
        ),
        check_vma=False,
    )
```

profile of v0, /device:TPU:0, one launch (start us, length us, event | category | flops | bytes accessed | tf_op | source)
XLA Modules:
  0.0 904.3 jit_solution(11059979735407355032)
XLA Ops:
  8.7 34.4 %all-gather.5.cloned.1.call-done = bf16[3,736,768]{1,2,0:T(8,128)(2,1)} async-done(((bf16[3,736,192]{1,2,0:T(8,128)(2,1)}), bf16[3,736,768]{1,2,0:T(8,128)(2,1)}) %all-gather.5.cloned.1.call-update) | async-done | bytes 3391504 | tf_op jit(solution)/shard_map/all_gather | solution.py:129
  43.1 6.1 copy.136
  53.5 5.9 fusion.66
  63.8 4.1 fusion.68
  79.6 25.4 %while.26 = (s32[]{:T(128)}, bf16[3,736,3,64]{1,3,2,0:T(8,128)(2,1)}, f32[3,3,736]{2,1,0:T(4,128)S(1)}, bf16[3,736,3,64]{1,3,2,0:T(8,128)(2,1)}, s32[3]{0:T(128)...) while((s32[]{:T(128)}, bf16[3,736,3,64]{1,3,2,0:T(8,128)(2,1)}, ...), condition=%wide.region_5.6_spmd, body=%wide.region_2.5_spmd.sunk | while | flops 436746816 | bytes 22955696 | solution.py:143
  84.0 4.0 fusion.156
  92.5 4.0 fusion.156
  101.0 4.0 fusion.156
  112.2 5.1 convolution_bitcast_fusion
  124.0 57.7 %reduce-scatter.7.cloned.1.call-done = f32[192,2208]{1,0:T(8,128)} async-done(((f32[768,2208]{1,0:T(8,128)}), f32[192,2208]{1,0:T(8,128)}) %reduce-scatter.7.cloned.1.call-update) | async-done | bytes 1695760
  193.3 21.9 %all-gather.7.cloned.1.call-done = bf16[2208,768]{0,1:T(8,128)(2,1)} async-done(((bf16[2208,192]{0,1:T(8,128)(2,1)}), bf16[2208,768]{0,1:T(8,128)(2,1)}) %all-gather.7.cloned.1.call-update) | async-done | bytes 3391504 | tf_op jit(solution)/shard_map/all_gather | solution.py:149
  215.2 5.7 copy.143
  225.3 5.5 fusion.79
  230.8 17.1 %all-gather.9.cloned.1.call-done = bf16[2208,768]{0,1:T(8,128)(2,1)} async-done(((bf16[2208,192]{0,1:T(8,128)(2,1)}), bf16[2208,768]{0,1:T(8,128)(2,1)}) %all-gather.9.cloned.1.call-update) | async-done | bytes 3391504 | tf_op jit(solution)/shard_map/all_gather | solution.py:167
  248.0 12.0 %convert_reduce_fusion.1 = (f32[768]{0:T(1024)}, bf16[2208,768]{1,0:T(8,128)(2,1)S(1)}, bf16[2208,768]{1,0:T(8,128)(2,1)}) fusion(f32[2208,768]{1,0:T(8,128)} %fusion.79, f32[768]{0:T(1024)S(1)} %copy-done.52, bf16[2208,768]{0,1:T(8,128)(2,1)} %all-gather.9.cloned.1.call-done, bf16[768,768]{1,0:T(8,128)(2,1)S(1)} %copy-done), kind=kOutput, calls=%fused_computation.80 | convolution fusion | flops 2647055616 | bytes 18143232 | tf_op jit(solution)/shard_map/dot_general | solution.py:25
  261.7 4.8 fusion.90
  268.5 125.8 %all-reduce.6.cloned.1.call-done = f32[2208,768]{1,0:T(8,128)} async-done(((f32[2208,768]{1,0:T(8,128)}), f32[2208,768]{1,0:T(8,128)}) %all-reduce.6.cloned.1.call-update) | async-done | bytes 6782992 | tf_op jit(solution)/shard_map/psum | solution.py:91
  394.2 6.3 fusion.86
  400.6 4.6 dynamic-slice_reduce_fusion
  408.6 15.8 %fusion.67 = bf16[768,2208]{1,0:T(8,128)(2,1)} fusion(bf16[2208,768]{1,0:T(8,128)(2,1)} %get-tuple-element.351, bf16[768,768]{1,0:T(8,128)(2,1)S(1)} %copy-done), kind=kOutput, calls=%fused_computation.92 | convolution fusion | flops 2606358528 | bytes 7962624 | tf_op jit(solution)/shard_map/dot_general | solution.py:15
  424.4 15.2 %all-gather.11.cloned.1.call-done = bf16[2208,768]{0,1:T(8,128)(2,1)} async-done(((bf16[2208,192]{0,1:T(8,128)(2,1)}), bf16[2208,768]{0,1:T(8,128)(2,1)}) %all-gather.11.cloned.1.call-update) | async-done | bytes 3391504 | tf_op jit(solution)/shard_map/all_gather | solution.py:178
  449.1 46.8 %while.27 = (s32[]{:T(128)}, bf16[3,736,3,64]{1,3,2,0:T(8,128)(2,1)}, bf16[3,736,3,64]{1,3,2,0:T(8,128)(2,1)}, bf16[3,736,3,64]{1,3,2,0:T(8,128)(2,1)}, bf16[3,7...) while((s32[]{:T(128)}, ...), condition=%wide.region_15.16_spmd, body=%wide.region_13.15_spmd.sunk | while | flops 1058095680 | bytes 86495392 | solution.py:182
  455.7 4.0 multiply_convert_fusion.3
  471.2 4.1 multiply_convert_fusion.3
  486.8 4.0 multiply_convert_fusion.3
  524.5 6.9 fusion.94
  531.4 4.9 fusion.78
  556.3 92.2 %all-reduce.8.cloned.1.call-done = f32[2208,768]{1,0:T(8,128)} async-done(((f32[2208,768]{1,0:T(8,128)}), f32[2208,768]{1,0:T(8,128)}) %all-reduce.8.cloned.1.call-update) | async-done | bytes 6782992 | tf_op jit(solution)/shard_map/psum | solution.py:91
  648.5 6.1 fusion.85
  654.6 4.8 dynamic-slice_reduce_fusion.1
  660.9 39.5 %all-reduce = (f32[192]{0:T(256)}, f32[192]{0:T(256)}, f32[192]{0:T(256)}, f32[192]{0:T(256)}, f32[192]{0:T(256)}, /*index=5*/f32[192]{0:T(256)}, f32[192]{0:T(256)}, f32[768]{0:T(1024)}, f32[192]{0:T(256)}) all-reduce(f32[192]{0:T(256)S(1)} %get-tuple-element.287, ...), channel_id=1, replica_groups=mesh['dp'=8,'tensor'=4] {'dp'}, use_global_device_ids=true, to_apply=%region_20.21 | all-reduce | flops 2304 | bytes 18432 | tf_op jit(solution)/shard_map/psum | solution.py:205
  700.3 187.3 %all-reduce.10.cloned.1.call-done = (f32[768,192]{0,1:T(8,128)}, f32[768,192]{0,1:T(8,128)}, f32[768,192]{0,1:T(8,128)}, f32[192,768]{1,0:T(8,128)}, f32[768,768]{1,0:T(8,128)}, /*index=5*/f32[768,768]{1,0:T(8,128)}) async-done(((f32[768,192]{0,1:T(8,128)}, f32[768,192]{0,1:T(8,128)}, f32[768,192]{0,1:T(8,128)}, f32[192,768]{1,0:T(8,128)}, f32[768,768]{1,0:T(8,128)}, /*index=5*/f32[768,768]{1,0:T(8,128)}), ...) | async-done | bytes 7077904 | tf_op jit(solution)/shard_map/psum | solution.py:205
  (265 shorter events, 175.9 us)
Async XLA Ops:
  7.2 240.8 %copy-start = (bf16[768,768]{1,0:T(8,128)(2,1)S(1)}, bf16[768,768]{1,0:T(8,128)(2,1)}, u32[]{:S(2)}) copy-start(bf16[768,768]{1,0:T(8,128)(2,1)} %param.37) | copy-start | bytes 3538948
  7.2 35.9 %all-gather.5.cloned.1.call-start = ((), (), s32[]{:S(2)}) async-start(), calls=%async_computation.2 | async-start | bytes 4423680 | tf_op jit(solution)/shard_map/all_gather | solution.py:129
  7.9 173.8 %reduce-scatter.7.cloned.1.call-start = ((), (), s32[]{:S(2)}) async-start(), calls=%async_computation.8 | async-start | bytes 8847360
  52.1 7.2 copy-start.32
  53.3 6.0 copy-start.34
  53.5 7.7 copy-start.28
  105.0 12.3 %copy-start.6 = (bf16[3,736,3,64]{1,3,2,0:T(8,128)(2,1)}, bf16[3,736,3,64]{1,3,2,0:T(8,128)(2,1)S(1)}, u32[]{:S(2)}) copy-start(bf16[3,736,3,64]{1,3,2,0:T(8,128)(2,1)S(1)} %get-tuple-element.572) | copy-start | bytes 2543620
  105.0 12.3 %copy-start.8 = (bf16[3,736,3,64]{1,3,2,0:T(8,128)(2,1)}, bf16[3,736,3,64]{1,3,2,0:T(8,128)(2,1)S(1)}, u32[]{:S(2)}) copy-start(bf16[3,736,3,64]{1,3,2,0:T(8,128)(2,1)S(1)} %get-tuple-element.573) | copy-start | bytes 2543620
  105.0 7.2 copy-start.23
  117.3 64.4 %copy-start.45 = (f32[192]{0:T(256)S(1)}, f32[192]{0:T(256)}, u32[]{:S(2)}) copy-start(f32[192]{0:T(256)} %param.32) | copy-start | bytes 2308
  117.4 97.8 %all-gather.7.cloned.1.call-start = ((), (), s32[]{:S(2)}) async-start(), calls=%async_computation.3 | async-start | bytes 4423680 | tf_op jit(solution)/shard_map/all_gather | solution.py:149
  124.0 62.4 %copy-start.10 = (f32[2208,192]{0,1:T(8,128)}, f32[2208,192]{0,1:T(8,128)S(1)}, u32[]{:S(2)}) copy-start(f32[2208,192]{0,1:T(8,128)S(1)} %reshape.324) | copy-start | bytes 5087236
  184.3 63.7 %all-gather.9.cloned.1.call-start = ((), (), s32[]{:S(2)}) async-start(), calls=%async_computation.4 | async-start | bytes 4423680 | tf_op jit(solution)/shard_map/all_gather | solution.py:167
  193.3 201.0 %all-reduce.6.cloned.1.call-start = ((), (), s32[]{:S(2)}) async-start(), calls=%async_computation.5 | async-start | bytes 13565952 | tf_op jit(solution)/shard_map/psum | solution.py:91
  225.3 22.7 %copy-start.52 = (f32[768]{0:T(1024)S(1)}, f32[768]{0:T(1024)}, u32[]{:S(2)}) copy-start(f32[768]{0:T(1024)} %param.36) | copy-start | bytes 9220
  248.0 13.7 %copy-start.51 = (bf16[768,768]{1,0:T(8,128)(2,1)S(1)}, bf16[768,768]{1,0:T(8,128)(2,1)}, u32[]{:S(2)}) copy-start(bf16[768,768]{1,0:T(8,128)(2,1)} %param.35) | copy-start | bytes 3538948
  266.5 173.1 %all-gather.11.cloned.1.call-start = ((), (), s32[]{:S(2)}) async-start(), calls=%async_computation.6 | async-start | bytes 4423680 | tf_op jit(solution)/shard_map/all_gather | solution.py:178
  394.2 6.3 copy-start.15
  408.5 135.7 %reduce-scatter.9.cloned.1.call-start = ((), (), s32[]{:S(2)}) async-start(), calls=%async_computation.9 | async-start | bytes 4423680
  424.4 15.3 %copy-start.24 = (bf16[192,768]{1,0:T(8,128)(2,1)S(1)}, bf16[192,768]{1,0:T(8,128)(2,1)}, u32[]{:S(2)}) copy-start(bf16[192,768]{1,0:T(8,128)(2,1)} %param.31) | copy-start | bytes 884740
  424.4 224.1 %all-reduce.8.cloned.1.call-start = ((), (), s32[]{:S(2)}) async-start(), calls=%async_computation.7 | async-start | bytes 13565952 | tf_op jit(solution)/shard_map/psum | solution.py:91
  504.3 10.0 %copy-start.27 = (bf16[768,192]{0,1:T(8,128)(2,1)S(1)}, bf16[768,192]{0,1:T(8,128)(2,1)}, u32[]{:S(2)}) copy-start(bf16[768,192]{0,1:T(8,128)(2,1)} %param.26) | copy-start | bytes 884740
  520.7 366.9 %all-reduce.10.cloned.1.call-start = ((), (), s32[]{:S(2)}) async-start(), calls=%async_computation.10 | async-start | bytes 14155776 | tf_op jit(solution)/shard_map/psum | solution.py:205
  524.4 6.9 copy-start.5
  524.5 6.9 copy-start.54
  524.5 6.9 copy-start.58
  544.2 10.4 %copy-start.16 = (bf16[3,736,3,64]{1,3,2,0:T(8,128)(2,1)S(1)}, bf16[3,736,3,64]{1,3,2,0:T(8,128)(2,1)}, u32[]{:S(2)}) copy-start(bf16[3,736,3,64]{1,3,2,0:T(8,128)(2,1)} %get-tuple-element.113) | copy-start | bytes 2543620
  648.5 6.1 copy-start.37
  654.6 6.2 copy-start.43
  654.6 6.2 copy-start.47
  887.6 6.1 copy-start.25
  887.6 6.9 copy-start.22
  (42 other events, 105.6 us)
Sparse Core Ops, SparseCore 0:
  9.6 33.4 all-gather.4
  117.5 64.1 reduce-scatter.6
  184.4 30.7 all-gather.6
  217.2 30.7 all-gather.8
  266.6 127.5 all-reduce.5
  408.7 30.9 all-gather.10
  442.2 40.3 reduce-scatter.8
  520.8 127.6 all-reduce.7
  654.7 232.8 all-reduce.9
where the time goes:
time: 915 us; the launch traced here: 904 us
  waiting for transfers between devices  552 us (60%)
  matrix products  125 us (14%)
  local copies, waits for them, and re-layouts  98.9 us (11%)
  other arithmetic  72.8 us (8%)
  blocking collectives  39.5 us (4%)
  between operations  14.9 us (2%)
    psum x2, waiting for transfers between devices, norm_back(): grad_norm = lax.psum(grad_part, 'tensor')  218 us
    psum x1, waiting for transfers between devices, local(): lax.psum((grad_attn_gain, grad_attn_shift, grad_query_weight, grad_key_we...  187 us
    unnamed x11, waiting for transfers between devices  58.5 us
    psum x1, blocking collectives, local(): lax.psum((grad_attn_gain, grad_attn_shift, grad_query_weight, grad_key_we...  39.5 us
    all_gather x1, waiting for transfers between devices, local(): lax.all_gather(tokens, 'tensor', axis=2, tiled=True).reshape(row_count, -1)  34.4 us
    dot_general x5, matrix products, matmul(): return jnp.dot(left, right, preferred_element_type=jnp.float32)  29.8 us
    dot_general x6, matrix products, times_transposed(): lax.dot_general(left, right, (((1,), (1,)), ((), ())), preferred_element_...  25.8 us
    all_gather x1, waiting for transfers between devices, local(): lax.all_gather(middle.astype(jnp.bfloat16), 'tensor', axis=1, tiled=True)  21.9 us
  transfers between devices with their start and end apart: 9, of which 8 were waited for; matrix products, arithmetic and copies ran while one was open for 19% of the time, Pallas kernels for 0%

commit v1 on v0

--- a/solution.py
+++ b/solution.py
@@ -88,7 +88,7 @@
 
 
 def norm_back(grad_part, normed, inv_std, gain, own_start, own_width):
-    grad_norm = lax.psum(grad_part, "tensor")
+    grad_norm = jnp.sum(lax.all_gather(grad_part, "tensor"), axis=0)
     scaled = grad_norm * gain
     first_mean = jnp.mean(scaled, axis=1, keepdims=True)
     second_mean = jnp.mean(scaled * normed, axis=1, keepdims=True)

time: 915 us -> 1050 us (1.15)
  waiting for transfers between devices: 552 us -> 665 us
  other arithmetic: 72.8 us -> 93.9 us
  local copies, waits for them, and re-layouts: 98.9 us -> 111 us
    all_gather x0 -> x2, waiting for transfers between devices: none -> 309 us  [norm_back(): grad_norm = jnp.sum(lax.all_gather(grad_part, 'tensor'), axis=0)]
    psum x2 -> x0, waiting for transfers between devices: 218 us -> none  [norm_back(): grad_norm = lax.psum(grad_part, 'tensor')]
    reduce_scatter x0 -> x2, waiting for transfers between devices: none -> 75.3 us  [the longest x1 56.5 us: local(): lax.psum_scatter(matmul(mixed, output_weight), 'tensor', scatter_dimensio...]
    unnamed x11 -> x9, waiting for transfers between devices: 58.5 us -> 0.81 us
    reduce_sum x0 -> x2, other arithmetic: none -> 26.7 us  [norm_back(): grad_norm = jnp.sum(lax.all_gather(grad_part, 'tensor'), axis=0)]
    all_gather x1, waiting for transfers between devices: 15.2 us -> 30.8 us  [local(): lax.all_gather(grad_middle.astype(jnp.bfloat16), 'tensor', axis=1, tiled=...]
    reduce_sum x0 -> x2, local copies, waits for them, and re-layouts: none -> 15.4 us  [norm_back(): grad_norm = jnp.sum(lax.all_gather(grad_part, 'tensor'), axis=0)]
    psum x1, waiting for transfers between devices: 187 us -> 173 us  [local(): lax.psum((grad_attn_gain, grad_attn_shift, grad_query_weight, grad_key_we...]
  transfers between devices with their start and end apart: 9 -> 9, of which waited for: 8 -> 9; matrix products, arithmetic and copies ran while one was open for 19% -> 10% of each run, Pallas kernels for 0% -> 0%
where the time goes in v1:
time: 1050 us; the launch traced here: 1040 us
  waiting for transfers between devices  665 us (63%)
  matrix products  117 us (11%)
  local copies, waits for them, and re-layouts  111 us (11%)
  other arithmetic  93.9 us (9%)
  blocking collectives  39.6 us (4%)
  between operations  14.9 us (1%)
    all_gather x2, waiting for transfers between devices, norm_back(): grad_norm = jnp.sum(lax.all_gather(grad_part, 'tensor'), axis=0)  309 us
    psum x1, waiting for transfers between devices, local(): lax.psum((grad_attn_gain, grad_attn_shift, grad_query_weight, grad_key_we...  173 us
    reduce_scatter x1, waiting for transfers between devices, local(): lax.psum_scatter(matmul(mixed, output_weight), 'tensor', scatter_dimensio...  56.5 us
    psum x1, blocking collectives, local(): lax.psum((grad_attn_gain, grad_attn_shift, grad_query_weight, grad_key_we...  39.6 us
    all_gather x1, waiting for transfers between devices, local(): lax.all_gather(tokens, 'tensor', axis=2, tiled=True).reshape(row_count, -1)  34.4 us
    all_gather x1, waiting for transfers between devices, local(): lax.all_gather(grad_middle.astype(jnp.bfloat16), 'tensor', axis=1, tiled=...  30.8 us
    reduce_sum x2, other arithmetic, norm_back(): grad_norm = jnp.sum(lax.all_gather(grad_part, 'tensor'), axis=0)  26.7 us
    dot_general x6, matrix products, times_transposed(): lax.dot_general(left, right, (((1,), (1,)), ((), ())), preferred_element_...  26 us
  transfers between devices with their start and end apart: 9, of which 9 were waited for; matrix products, arithmetic and copies ran while one was open for 10% of the time, Pallas kernels for 0%

profile of v1, /device:TPU:0, one launch (start us, length us, event | category | flops | bytes accessed | tf_op | source)
XLA Modules:
  0.0 1042.9 jit_solution(17749332798230605925)
XLA Ops:
  8.7 34.4 %all-gather.9.cloned.1.call-done = bf16[3,736,768]{1,2,0:T(8,128)(2,1)} async-done(((bf16[3,736,192]{1,2,0:T(8,128)(2,1)}), bf16[3,736,768]{1,2,0:T(8,128)(2,1)}) %all-gather.9.cloned.1.call-update) | async-done | bytes 3391504 | tf_op jit(solution)/shard_map/all_gather | solution.py:129
  43.1 6.0 copy.79
  53.4 5.9 copy.80
  59.4 5.7 add_convert_fusion.1
  84.1 25.6 %while.26 = (s32[]{:T(128)}, bf16[3,736,3,64]{1,3,2,0:T(8,128)(2,1)}, f32[3,3,736]{2,1,0:T(4,128)S(1)}, bf16[3,736,3,64]{1,3,2,0:T(8,128)(2,1)}, s32[3]{0:T(128)...) while((s32[]{:T(128)}, bf16[3,736,3,64]{1,3,2,0:T(8,128)(2,1)}, ...), condition=%wide.region_5.6_spmd, body=%wide.region_2.5_spmd.sunk | while | flops 436746816 | bytes 22955696 | solution.py:143
  116.4 5.2 fusion.85
  124.9 4.5 reshape.345
  129.4 56.5 %reduce-scatter.3.cloned.1.call-done = f32[2208,192]{0,1:T(8,128)} async-done(((f32[2208,768]{0,1:T(8,128)}), f32[2208,192]{0,1:T(8,128)}) %reduce-scatter.3.cloned.1.call-update) | async-done | bytes 1695760 | tf_op jit(solution)/shard_map/reduce_scatter | solution.py:145
  192.6 4.3 reshape.339
  199.9 20.0 %all-gather.11.cloned.1.call-done = bf16[2208,768]{0,1:T(8,128)(2,1)} async-done(((bf16[2208,192]{0,1:T(8,128)(2,1)}), bf16[2208,768]{0,1:T(8,128)(2,1)}) %all-gather.11.cloned.1.call-update) | async-done | bytes 3391504 | tf_op jit(solution)/shard_map/all_gather | solution.py:149
  224.0 6.2 fusion.79
  230.2 22.5 %all-gather.13.cloned.1.call-done = bf16[2208,768]{0,1:T(8,128)(2,1)} async-done(((bf16[2208,192]{0,1:T(8,128)(2,1)}), bf16[2208,768]{0,1:T(8,128)(2,1)}) %all-gather.13.cloned.1.call-update) | async-done | bytes 3391504 | tf_op jit(solution)/shard_map/all_gather | solution.py:167
  252.7 12.2 %convert_reduce_fusion.1 = (f32[768]{0:T(1024)}, bf16[2208,768]{1,0:T(8,128)(2,1)S(1)}, bf16[2208,768]{1,0:T(8,128)(2,1)}) fusion(f32[2208,768]{1,0:T(8,128)} %fusion.79, f32[768]{0:T(1024)S(1)} %copy-done.53, bf16[2208,768]{0,1:T(8,128)(2,1)} %all-gather.13.cloned.1.call-done, bf16[768,768]{1,0:T(8,128)(2,1)S(1)} %copy-done), kind=kOutput, calls=%fused_computation.82 | convolution fusion | flops 2647055616 | bytes 18143232 | tf_op jit(solution)/shard_map/dot_general | solution.py:25
  266.7 4.8 fusion.86
  271.6 165.8 %all-gather.17.cloned.1.call-done = f32[8832,768]{1,0:T(8,128)} async-done(((f32[2208,768]{1,0:T(8,128)}), f32[8832,768]{1,0:T(8,128)}) %all-gather.17.cloned.1.call-update) | async-done | bytes 27131920 | tf_op jit(solution)/shard_map/all_gather | solution.py:91
  437.3 12.9 %reduce_sum.199 = f32[2208,768]{1,0:T(8,128)} reduce(f32[4,2208,768]{2,1,0:T(8,128)} %bitcast.177, f32[]{:T(128)} %constant.71.clone.1), dimensions={0}, to_apply=%region_10.11 | reduce | flops 5087232 | bytes 33914884 | tf_op jit(solution)/shard_map/reduce_sum | solution.py:91
  450.3 7.7 copy.86
  458.0 5.2 fusion.80
  468.6 30.8 %all-gather.15.cloned.1.call-done = bf16[2208,768]{0,1:T(8,128)(2,1)} async-done(((bf16[2208,192]{0,1:T(8,128)(2,1)}), bf16[2208,768]{0,1:T(8,128)(2,1)}) %all-gather.15.cloned.1.call-update) | async-done | bytes 3391504 | tf_op jit(solution)/shard_map/all_gather | solution.py:178
  509.1 46.7 %while.27 = (s32[]{:T(128)}, bf16[3,736,3,64]{1,3,2,0:T(8,128)(2,1)}, bf16[3,736,3,64]{1,3,2,0:T(8,128)(2,1)}, bf16[3,736,3,64]{1,3,2,0:T(8,128)(2,1)}, bf16[3,7...) while((s32[]{:T(128)}, ...), condition=%wide.region_15.16_spmd, body=%wide.region_13.15_spmd.sunk | while | flops 1058095680 | bytes 83103872 | solution.py:182
  515.6 4.0 multiply_convert_fusion.3
  531.2 4.0 multiply_convert_fusion.3
  578.8 6.4 convolution_convert_fusion
  585.3 9.4 fusion.90
  594.7 4.9 fusion.78
  601.7 142.8 %all-gather.19.cloned.1.call-done = f32[8832,768]{1,0:T(8,128)} async-done(((f32[2208,768]{1,0:T(8,128)}), f32[8832,768]{1,0:T(8,128)}) %all-gather.19.cloned.1.call-update) | async-done | bytes 27131920 | tf_op jit(solution)/shard_map/all_gather | solution.py:91
  744.5 13.8 %reduce_sum.202 = f32[2208,768]{1,0:T(8,128)} reduce(f32[4,2208,768]{2,1,0:T(8,128)} %bitcast.176, f32[]{:T(128)} %constant.71.clone.1), dimensions={0}, to_apply=%region_16.17 | reduce | flops 5087232 | bytes 33914884 | tf_op jit(solution)/shard_map/reduce_sum | solution.py:91
  758.3 5.3 add_convert_fusion.2
  768.7 18.8 %reduce-scatter.5.cloned.1.call-done = bf16[2208,192]{0,1:T(8,128)(2,1)} async-done(((bf16[2208,768]{0,1:T(8,128)(2,1)}), bf16[2208,192]{0,1:T(8,128)(2,1)}) %reduce-scatter.5.cloned.1.call-update) | async-done | bytes 847888 | tf_op jit(solution)/shard_map/reduce_scatter | solution.py:157
  797.1 7.7 copy.94
  813.9 39.6 %all-reduce = (f32[192]{0:T(256)}, f32[192]{0:T(256)}, f32[192]{0:T(256)}, f32[192]{0:T(256)}, f32[192]{0:T(256)}, /*index=5*/f32[192]{0:T(256)}, f32[192]{0:T(256)}, f32[768]{0:T(1024)}, f32[192]{0:T(256)}) all-reduce(f32[192]{0:T(256)S(1)} %get-tuple-element.219, ...), channel_id=1, replica_groups=mesh['dp'=8,'tensor'=4] {'dp'}, use_global_device_ids=true, to_apply=%region_20.21 | all-reduce | flops 2304 | bytes 18432 | tf_op jit(solution)/shard_map/psum | solution.py:205
  853.5 172.8 %all-reduce.4.cloned.1.call-done = (f32[768,192]{0,1:T(8,128)}, f32[768,192]{0,1:T(8,128)}, f32[768,192]{0,1:T(8,128)}, f32[192,768]{1,0:T(8,128)}, f32[768,768]{1,0:T(8,128)}, /*index=5*/f32[768,768]{1,0:T(8,128)}) async-done(((f32[768,192]{0,1:T(8,128)}, f32[768,192]{0,1:T(8,128)}, f32[768,192]{0,1:T(8,128)}, f32[192,768]{1,0:T(8,128)}, f32[768,768]{1,0:T(8,128)}, /*index=5*/f32[768,768]{1,0:T(8,128)}), ...) | async-done | bytes 7077904 | tf_op jit(solution)/shard_map/psum | solution.py:205
  (267 shorter events, 187.4 us)
Async XLA Ops:
  7.2 245.5 %copy-start = (bf16[768,768]{1,0:T(8,128)(2,1)S(1)}, bf16[768,768]{1,0:T(8,128)(2,1)}, u32[]{:S(2)}) copy-start(bf16[768,768]{1,0:T(8,128)(2,1)} %param.37) | copy-start | bytes 3538948
  7.2 35.9 %all-gather.9.cloned.1.call-start = ((), (), s32[]{:S(2)}) async-start(), calls=%async_computation.2 | async-start | bytes 4423680 | tf_op jit(solution)/shard_map/all_gather | solution.py:129
  7.9 178.0 %reduce-scatter.3.cloned.1.call-start = ((), (), s32[]{:S(2)}) async-start(), calls=%async_computation.3 | async-start | bytes 8847360 | tf_op jit(solution)/shard_map/reduce_scatter | solution.py:145
  52.1 7.3 copy-start.31
  59.4 7.4 copy-start.29
  59.4 7.4 copy-start.56
  109.7 11.8 %copy-start.5 = (bf16[3,736,3,64]{1,3,2,0:T(8,128)(2,1)}, bf16[3,736,3,64]{1,3,2,0:T(8,128)(2,1)S(1)}, u32[]{:S(2)}) copy-start(bf16[3,736,3,64]{1,3,2,0:T(8,128)(2,1)S(1)} %get-tuple-element.509) | copy-start | bytes 2543620
  121.6 64.4 %copy-start.44 = (f32[192]{0:T(256)S(1)}, f32[192]{0:T(256)}, u32[]{:S(2)}) copy-start(f32[192]{0:T(256)} %param.32) | copy-start | bytes 2308
  121.6 98.4 %all-gather.11.cloned.1.call-start = ((), (), s32[]{:S(2)}) async-start(), calls=%async_computation.4 | async-start | bytes 4423680 | tf_op jit(solution)/shard_map/all_gather | solution.py:149
  129.4 59.8 %copy-start.25 = (bf16[3,736,192]{1,2,0:T(8,128)(2,1)S(1)}, bf16[3,736,192]{1,2,0:T(8,128)(2,1)}, u32[]{:S(2)}) copy-start(bf16[3,736,192]{1,2,0:T(8,128)(2,1)} %param.39) | copy-start | bytes 2543620
  189.1 63.7 %all-gather.13.cloned.1.call-start = ((), (), s32[]{:S(2)}) async-start(), calls=%async_computation.6 | async-start | bytes 4423680 | tf_op jit(solution)/shard_map/all_gather | solution.py:167
  199.8 24.1 %copy-start.43 = (f32[768]{0:T(1024)S(1)}, f32[768]{0:T(1024)}, u32[]{:S(2)}) copy-start(f32[768]{0:T(1024)} %param.33) | copy-start | bytes 9220
  199.9 24.1 %copy-start.54 = (f32[768]{0:T(1024)S(1)}, f32[768]{0:T(1024)}, u32[]{:S(2)}) copy-start(f32[768]{0:T(1024)} %param.34) | copy-start | bytes 9220
  199.9 237.5 %all-gather.17.cloned.1.call-start = ((), (), s32[]{:S(2)}) async-start(), calls=%async_computation.8 | async-start | bytes 33914880 | tf_op jit(solution)/shard_map/all_gather | solution.py:91
  224.0 28.7 %copy-start.53 = (f32[768]{0:T(1024)S(1)}, f32[768]{0:T(1024)}, u32[]{:S(2)}) copy-start(f32[768]{0:T(1024)} %param.36) | copy-start | bytes 9220
  252.7 14.0 %copy-start.52 = (bf16[768,768]{1,0:T(8,128)(2,1)S(1)}, bf16[768,768]{1,0:T(8,128)(2,1)}, u32[]{:S(2)}) copy-start(bf16[768,768]{1,0:T(8,128)(2,1)} %param.35) | copy-start | bytes 3538948
  271.5 227.9 %all-gather.15.cloned.1.call-start = ((), (), s32[]{:S(2)}) async-start(), calls=%async_computation.7 | async-start | bytes 4423680 | tf_op jit(solution)/shard_map/all_gather | solution.py:178
  468.6 276.0 %all-gather.19.cloned.1.call-start = ((), (), s32[]{:S(2)}) async-start(), calls=%async_computation.9 | async-start | bytes 33914880 | tf_op jit(solution)/shard_map/all_gather | solution.py:91
  563.2 9.2 copy-start.24
  578.7 208.8 %reduce-scatter.5.cloned.1.call-start = ((), (), s32[]{:S(2)}) async-start(), calls=%async_computation.5 | async-start | bytes 4423680 | tf_op jit(solution)/shard_map/reduce_scatter | solution.py:157
  585.2 9.5 copy-start.55
  585.2 441.1 %all-reduce.4.cloned.1.call-start = ((), (), s32[]{:S(2)}) async-start(), calls=%async_computation.10 | async-start | bytes 14155776 | tf_op jit(solution)/shard_map/psum | solution.py:205
  585.3 9.4 copy-start.4
  585.3 9.4 copy-start.59
  744.5 13.8 %copy-start.32 = (f32[3,736]{1,0:T(4,128)S(1)}, f32[3,736]{1,0:T(4,128)}, u32[]{:S(2)}) copy-start(f32[3,736]{1,0:T(4,128)} %copy-done.31) | copy-start | bytes 26500
  744.5 13.8 %copy-start.36 = (f32[3,736]{1,0:T(4,128)S(1)}, f32[3,736]{1,0:T(4,128)}, u32[]{:S(2)}) copy-start(f32[3,736]{1,0:T(4,128)} %copy-done.35) | copy-start | bytes 26500
  744.5 13.8 %copy-start.39 = (f32[768]{0:T(1024)S(1)}, f32[768]{0:T(1024)}, u32[]{:S(2)}) copy-start(f32[768]{0:T(1024)} %param.24) | copy-start | bytes 9220
  744.5 13.8 %copy-start.41 = (f32[768]{0:T(1024)S(1)}, f32[768]{0:T(1024)}, u32[]{:S(2)}) copy-start(f32[768]{0:T(1024)} %param.25) | copy-start | bytes 9220
  768.7 18.8 %copy-start.7 = (f32[2208,192]{0,1:T(8,128)S(1)}, f32[2208,192]{0,1:T(8,128)}, u32[]{:S(2)}) copy-start(f32[2208,192]{0,1:T(8,128)} %reshape.345) | copy-start | bytes 5087236
  768.7 18.8 %copy-start.45 = (f32[192]{0:T(256)S(1)}, f32[192]{0:T(256)}, u32[]{:S(2)}) copy-start(f32[192]{0:T(256)} %param.32) | copy-start | bytes 2308
  768.7 18.8 %copy-start.50 = (f32[192]{0:T(256)S(1)}, f32[192]{0:T(256)}, u32[]{:S(2)}) copy-start(f32[192]{0:T(256)} %param.38) | copy-start | bytes 2308
  1026.3 6.9 copy-start.21
  (41 other events, 150.0 us)
Sparse Core Ops, SparseCore 0:
  9.6 33.4 all-gather.8
  121.7 64.1 reduce-scatter.2
  189.2 30.7 all-gather.10
  221.9 30.7 all-gather.12
  271.6 165.6 all-gather.16
  468.7 30.7 all-gather.14
  578.8 165.6 all-gather.18
  747.1 40.3 reduce-scatter.4
  793.7 232.5 all-reduce.3
